TPU v7x, 256 devices: a whole 4x4x8 slice. The times are simulated.
256 devices in a mesh: pts: 64 (over x, z, core), rep: 4 (over y).
Axes of the slice: x: 4, y: 4, z: 8, core: 2. Of those that a mesh axis runs over, the one named last changes fastest.
Arguments:
- points: bfloat16 [4, 131072, 512], P('rep', 'pts'), may hold values from -60 to 60
- counts: int32 [4, 64], P('rep', 'pts'), may hold values from 0 to 2048, as said below
- hilbert_rank: int32 [4, 131072], P('rep', 'pts'), may hold values from 0 to 65535, as said below
- patch_shift: int32 [4], P('rep'), may hold values from 1 to 1023
- norm_gain: float32 [512], replicated, may hold values from 0.1 to 1.9
- project_in: bfloat16 [512, 1536], replicated, may hold values from -8 to 8
- project_out: bfloat16 [512, 512], replicated, may hold values from -0.25 to 0.25
- cotangent: bfloat16 [4, 65536, 512], P('rep', 'pts'), may hold values from -6 to 6
Outputs:
- block_out: bfloat16 [4, 65536, 512], P('rep', 'pts')
- grad_points: bfloat16 [4, 131072, 512], P('rep', 'pts')
- grad_project_in: float32 [512, 1536], replicated
- grad_project_out: float32 [512, 512], replicated
- grad_gain: float32 [512], replicated
Inputs may be any that keep to these rules, and one draw needn't show every extreme that they name: The valid points of shard d fill its first counts[b, d] slots; the counts of a scan sum to 65536, and in every scan some shard holds exactly 2048. `hilbert_rank`: the ranks of the valid slots of a scan are a permutation of 0 to 65535. At most 32 valid slots of one shard have ranks in one block [m * 1024, (m + 1) * 1024); in every scan some shard has exactly 32 in every block. Slots beyond the count hold arbitrary ranks.
All inputs are finite; a program needn't handle non-finite values.
Results may differ from a plain program's by a relative error of at most 0.012.
The roundings to bfloat16 on the way count: a program that leaves them out, or rounds other values in their place, can miss the bound.
Values may be sent and summed in bfloat16 or wider, within the bound.
A program may use at most 128 MiB of HBM per device.

v0:
```python
import math
import jax
import jax.numpy as jnp
from jax import lax
from jax.sharding import PartitionSpec as P

HEAD_DIM = 64
PATCH = 1024
EPSILON = 1e-05


def shifted(value, axis, steps):
    count = lax.axis_size(axis)
    pairs = [(source, (source + steps) % count) for source in range(count)]
    return lax.ppermute(value, axis, pairs)


def layer_stats(rows_in):
    values = rows_in.astype(jnp.float32)
    centre = jnp.mean(values, axis=-1, keepdims=True)
    deviation = values - centre
    inverse = lax.rsqrt(jnp.mean(deviation * deviation, axis=-1, keepdims=True) + EPSILON)
    return (deviation * inverse, inverse)


def split_heads(projected):
    row_count = projected.shape[0]
    head_count = projected.shape[1] // (3 * HEAD_DIM)
    shaped = projected.reshape(row_count // PATCH, PATCH, 3, head_count, HEAD_DIM)
    return jnp.transpose(shaped, (2, 3, 0, 1, 4))


def join_heads(per_head):
    head_count, group_count, patch_rows, depth = per_head.shape
    return jnp.transpose(per_head, (1, 2, 0, 3)).reshape(
        group_count * patch_rows, head_count * depth
    )


def head_forward(triple):
    queries, key_rows, value_rows = triple
    logits = jnp.einsum(
        "gqd,gkd->gqk", queries, key_rows, preferred_element_type=jnp.float32
    ) * HEAD_DIM ** (-0.5)
    attention = jax.nn.softmax(logits, axis=-1).astype(jnp.bfloat16)
    return jnp.einsum(
        "gqk,gkd->gqd", attention, value_rows, preferred_element_type=jnp.float32
    ).astype(jnp.bfloat16)


def attend_forward(projected):
    parts = split_heads(projected)
    return join_heads(lax.map(head_forward, (parts[0], parts[1], parts[2])))


def head_backward(quadruple):
    queries, key_rows, value_rows, grad_rows = quadruple
    logits = jnp.einsum(
        "gqd,gkd->gqk", queries, key_rows, preferred_element_type=jnp.float32
    ) * HEAD_DIM ** (-0.5)
    attention_f32 = jax.nn.softmax(logits, axis=-1)
    attention = attention_f32.astype(jnp.bfloat16)
    grad_values = jnp.einsum(
        "gqk,gqd->gkd", attention, grad_rows, preferred_element_type=jnp.float32
    ).astype(jnp.bfloat16)
    grad_attention = jnp.einsum(
        "gqd,gkd->gqk", grad_rows, value_rows, preferred_element_type=jnp.float32
    )
    row_dot = jnp.sum(grad_attention * attention_f32, axis=-1, keepdims=True)
    grad_logits = (attention_f32 * (grad_attention - row_dot) * HEAD_DIM ** (-0.5)).astype(
        jnp.bfloat16
    )
    grad_queries = jnp.einsum(
        "gqk,gkd->gqd", grad_logits, key_rows, preferred_element_type=jnp.float32
    ).astype(jnp.bfloat16)
    grad_keys = jnp.einsum(
        "gqk,gqd->gkd", grad_logits, queries, preferred_element_type=jnp.float32
    ).astype(jnp.bfloat16)
    return jnp.stack([grad_queries, grad_keys, grad_values])


def attend_backward(projected, grad_mixed):
    parts = split_heads(projected)
    row_count = projected.shape[0]
    head_count = parts.shape[1]
    grad_parts = jnp.transpose(
        grad_mixed.reshape(row_count // PATCH, PATCH, head_count, HEAD_DIM), (2, 0, 1, 3)
    )
    stacked = lax.map(head_backward, (parts[0], parts[1], parts[2], grad_parts))
    return jnp.transpose(stacked, (2, 3, 1, 0, 4)).reshape(row_count, 3 * head_count * HEAD_DIM)


def route_slots(rank_row, point_count, total, row_count, shard_count, send_size):
    slot_total = rank_row.shape[0]
    live_slot = jnp.arange(slot_total, dtype=jnp.int32) < point_count
    moved = rank_row % total
    target_shard = jnp.where(live_slot, moved // row_count, shard_count)
    matches = (target_shard[:, None] == jnp.arange(shard_count, dtype=jnp.int32)[None, :]).astype(
        jnp.int32
    )
    ordinal = jnp.sum((jnp.cumsum(matches, axis=0) - 1) * matches, axis=1)
    target = jnp.where(live_slot, target_shard * send_size + ordinal, shard_count * send_size)
    return (live_slot, target, moved % row_count)


def on_device(
    points, counts, hilbert_rank, patch_shift, norm_gain, project_in, project_out, cotangent
):
    shard_count = lax.axis_size("pts")
    row_count = cotangent.shape[1]
    width = points.shape[2]
    slot_size = points.shape[1] // shard_count
    total = row_count * shard_count
    offset = patch_shift[0]
    live_slot, target, position = route_slots(
        hilbert_rank[0], counts[0, 0], total, row_count, shard_count, slot_size
    )
    outgoing = (
        jnp.zeros((shard_count * slot_size, width), jnp.bfloat16)
        .at[target]
        .set(points[0], mode="drop")
    )
    out_position = (
        jnp.full((shard_count * slot_size,), -1, jnp.int32).at[target].set(position, mode="drop")
    )
    incoming, in_position = (
        lax.all_to_all(outgoing, "pts", split_axis=0, concat_axis=0, tiled=True),
        lax.all_to_all(out_position, "pts", split_axis=0, concat_axis=0, tiled=True),
    )
    placed = jnp.where(in_position < 0, row_count, in_position)
    ordered = jnp.zeros((row_count, width), jnp.bfloat16).at[placed].set(incoming, mode="drop")
    unit_rows, inverse = layer_stats(ordered)
    normed = (unit_rows * norm_gain).astype(jnp.bfloat16)
    projected = jnp.dot(normed, project_in, preferred_element_type=jnp.float32).astype(jnp.bfloat16)
    cot_rows = cotangent[0]
    next_rows = shifted(projected, "pts", -1)
    window_in = lax.dynamic_slice_in_dim(
        jnp.concatenate([projected, next_rows], axis=0), offset, row_count, 0
    )
    window_mixed = attend_forward(window_in)
    tail_rows = shifted(window_mixed, "pts", 1)
    mixed_rows = lax.dynamic_slice_in_dim(
        jnp.concatenate([tail_rows, window_mixed], axis=0), PATCH - offset, row_count, 0
    )
    block_rows = (
        ordered.astype(jnp.float32)
        + jnp.dot(mixed_rows, project_out, preferred_element_type=jnp.float32)
    ).astype(jnp.bfloat16)
    grad_mixed = jnp.dot(cot_rows, project_out.T, preferred_element_type=jnp.float32).astype(
        jnp.bfloat16
    )
    grad_out = jnp.dot(mixed_rows.T, cot_rows, preferred_element_type=jnp.float32)
    next_grads = shifted(grad_mixed, "pts", -1)
    window_grad = lax.dynamic_slice_in_dim(
        jnp.concatenate([grad_mixed, next_grads], axis=0), offset, row_count, 0
    )
    grad_window = attend_backward(window_in, window_grad)
    spread = lax.dynamic_update_slice(
        jnp.zeros((row_count + PATCH, 3 * width), jnp.bfloat16), grad_window, (offset, jnp.int32(0))
    )
    returned = shifted(spread[row_count:], "pts", 1)
    grad_projected = spread[:row_count].at[:PATCH].add(returned)
    grad_in = jnp.dot(normed.T, grad_projected, preferred_element_type=jnp.float32)
    grad_normed = jnp.dot(grad_projected, project_in.T, preferred_element_type=jnp.float32)
    grad_scale = jnp.sum(grad_normed * unit_rows, axis=0)
    weighted = grad_normed * norm_gain
    branch = inverse * (
        weighted
        - jnp.mean(weighted, axis=-1, keepdims=True)
        - unit_rows * jnp.mean(weighted * unit_rows, axis=-1, keepdims=True)
    )
    grad_ordered = (cot_rows.astype(jnp.float32) + branch).astype(jnp.bfloat16)
    safe_position = jnp.clip(in_position, 0, row_count - 1)
    returning = jnp.where(
        in_position[:, None] >= 0, grad_ordered[safe_position], jnp.zeros((), jnp.bfloat16)
    )
    arrived = lax.all_to_all(returning, "pts", split_axis=0, concat_axis=0, tiled=True)
    safe_target = jnp.clip(target, 0, shard_count * slot_size - 1)
    grad_points = jnp.where(live_slot[:, None], arrived[safe_target], jnp.zeros((), jnp.bfloat16))
    summed_in, summed_out, summed_scale = lax.psum((grad_in, grad_out, grad_scale), ("pts", "rep"))
    factor = 1.0 / math.sqrt(total * lax.axis_size("rep"))
    return (
        block_rows[None],
        grad_points[None],
        summed_in * factor,
        summed_out * factor,
        summed_scale * factor,
    )


def solution(mesh):
    return jax.shard_map(
        on_device,
        mesh=mesh,
        in_specs=(
            P("rep", "pts", None),
            P("rep", "pts"),
            P("rep", "pts"),
            P("rep"),
            P(),
            P(),
            P(),
            P("rep", "pts", None),
        ),
        out_specs=(P("rep", "pts", None), P("rep", "pts", None), P(), P(), P()),
        check_vma=False,
    )
```

profile of v0, /device:TPU:97, one launch (start us, length us, event | category | flops | bytes accessed | tf_op | source)
XLA Modules:
  0.0 731.6 jit_solution(16514262569084634420)
XLA Ops:
  8.8 18.1 %reduce-window.6 = s32[64,16,128]{2,1,0:T(8,128)S(1)} reduce-window(s32[64,16,128]{2,1,0:T(8,128)S(1)} %fusion.81, s32[]{:T(128)} %constant.143.clone.1), window={size=1x1x128 pad=0_0x0_0x127_0}, to_apply=%region_0.1 | reduce-window | flops 16646144 | bytes 1048580 | tf_op jit(solution)/shard_map/reduce-window
  28.9 8.0 %scatter_custom_fusion = s32[2048]{0:T(1024)S(1)} fusion(s32[2048]{0:T(1024)S(1)} %bitcast.195, s32[2048]{0:T(1024)S(1)} %get-tuple-element.159, s32[]{:T(128)} %constant.142.clone.1), kind=kCustom, calls=%fused_computation.164 | custom fusion | bytes 8196 | tf_op jit(solution)/shard_map/scatter | solution.py:124
  37.6 11.0 %all-to-all-start = ((s32[64,32,1]{1,2,0:T(1,128)}), s32[64,32,1]{1,2,0:T(1,128)S(1)}, u32[]{:S(2)}, u32[]{:S(2)}) async-start(s32[64,32,1]{1,2,0:T(1,128)} %bitcast.21), calls=%async_computation | async-start | bytes 65536 | tf_op jit(solution)/shard_map/all_to_all | solution.py:128
  48.6 11.0 %scatter_custom_fusion.1 = bf16[2048,512]{1,0:T(8,128)(2,1)} fusion(s32[2048]{0:T(1024)S(1)} %bitcast.196, bf16[1,2048,512]{2,1,0:T(8,128)(2,1)S(1)} %copy-done, bf16[]{:T(256)} %constant.141.clone.1), kind=kCustom, calls=%fused_computation.88 | custom fusion | bytes 4194306 | tf_op jit(solution)/shard_map/scatter | solution.py:121
  59.6 10.3 %all-to-all-start.1 = ((bf16[64,32,512]{2,1,0:T(8,128)(2,1)}), bf16[64,32,512]{2,1,0:T(8,128)(2,1)S(1)}, u32[]{:S(2)}, u32[]{:S(2)}) async-start(bf16[64,32,512]{2,1,0:T(8,128)(2,1)} %bitcast.182), calls=%async_computation.1 | async-start | bytes 4194304 | tf_op jit(solution)/shard_map/all_to_all | solution.py:127
  71.3 47.5 %all-to-all-done.1 = bf16[64,32,512]{2,1,0:T(8,128)(2,1)S(1)} async-done(((bf16[64,32,512]{2,1,0:T(8,128)(2,1)}), bf16[64,32,512]{2,1,0:T(8,128)(2,1)S(1)}, u32[]{:S(2)}, u32[]{:S(2)}) %all-to-all-start.1) | async-done | bytes 2097184 | tf_op jit(solution)/shard_map/all_to_all | solution.py:127
  118.8 22.3 %scatter_custom_fusion.2 = bf16[1024,512]{1,0:T(8,128)(2,1)S(1)} fusion(s32[2048]{0:T(1024)S(1)} %bitcast.194, bf16[2048,512]{1,0:T(8,128)(2,1)S(1)} %bitcast.184, bf16[]{:T(256)} %constant.141.clone.1), kind=kCustom, calls=%fused_computation.113 | custom fusion | bytes 1048578 | tf_op jit(solution)/shard_map/scatter | solution.py:131
  142.5 3.5 convolution_convert_fusion.2
  149.2 46.3 %collective-permute-done.2 = bf16[1024,512]{1,0:T(8,128)(2,1)} collective-permute-done((bf16[1024,512]{1,0:T(8,128)(2,1)S(1)}, bf16[1024,512]{1,0:T(8,128)(2,1)}, u32[]{:S(2)}, u32[]{:S(2)}) %collective-permute-start.2) | collective-permute-done | bytes 1048608 | tf_op jit(solution)/shard_map/ppermute | solution.py:15
  195.5 2.6 fusion.69
  199.5 6.7 fusion.50
  206.2 4.6 copy.47
  210.9 3.7 slice_bitcast_fusion
  218.3 2.7 copy.48
  221.0 85.2 %while.23 = (s32[]{:T(128)}, bf16[8,3,1,1024,64]{3,4,0,1,2:T(8,128)(2,1)}, bf16[8,1,1024,64]{3,2,1,0:T(8,128)(2,1)}, bf16[8,1,1024,64]{3,2,1,0:T(8,128)(2,1)S(1)...) while((s32[]{:T(128)}, bf16[8,3,1,1024,64]{3,4,0,1,2:T(8,128)(2,1)}, ...), condition=%wide.region_16.17_spmd, body=%wide.region_12.16_spmd.sunk | while | flops 694481920 | bytes 38451300 | solution.py:89
  225.3 2.0 multiply_reduce_fusion.9
  236.0 2.0 multiply_reduce_fusion.9
  246.6 2.0 multiply_reduce_fusion.9
  257.3 2.0 multiply_reduce_fusion.9
  267.9 2.0 multiply_reduce_fusion.9
  278.5 2.0 multiply_reduce_fusion.9
  289.2 2.0 multiply_reduce_fusion.9
  299.8 2.0 multiply_reduce_fusion.9
  306.2 3.5 broadcast_in_dim.94
  309.6 31.6 %dynamic_update_slice.11 = bf16[2048,1536]{0,1:T(8,128)(2,1)} dynamic-update-slice(bf16[2048,1536]{0,1:T(8,128)(2,1)} %broadcast_in_dim.94, bf16[1024,1536]{0,1:T(8,128)(2,1)} %bitcast.183, s32[]{:T(128)S(6)} %select_n.180, s32[]{:T(128)} %constant.143.clone.1) | dynamic-update-slice | bytes 6291460 | tf_op jit(solution)/shard_map/dynamic_update_slice | solution.py:158
  341.3 3.9 slice.55
  345.1 40.1 %while.22 = (s32[]{:T(128)}, bf16[8,1,1024,64]{2,3,1,0:T(8,128)(2,1)}, bf16[8,1,1024,64]{3,2,1,0:T(8,128)(2,1)}, bf16[8,1,1024,64]{3,2,1,0:T(8,128)(2,1)S(1)}, bf16[8,1,1024,64]{3,2,1,0:T(8,128)(2,1)}, /*index=5*/s32[]{:T(128)}) while((s32[]{:T(128)}, bf16[8,1,1024,64]{2,3,1,0:T(8,128)(2,1)}, bf16[8,1,1024,64]{3,2,1,0:T(8,128)(2,1)}, ...), condition=%wide.region_11.12_spmd, body=%wide.region_8.11_spmd.sunk | while | flops 277936128 | bytes 13523021 | solution.py:53
  347.5 2.6 fusion.121
  352.5 2.6 fusion.121
  357.6 2.6 fusion.121
  362.6 2.6 fusion.121
  367.6 2.6 fusion.121
  372.6 2.6 fusion.121
  377.6 2.6 fusion.121
  382.6 2.6 fusion.121
  386.1 5.2 fusion.63
  392.4 9.2 %gather_fusion = bf16[2048,512]{1,0:T(8,128)(2,1)} fusion(bf16[1024,512]{1,0:T(8,128)(2,1)S(1)} %fusion.62, s32[2048]{0:T(1024)S(1)} %copy-done.6), kind=kCustom, calls=%fused_computation | custom fusion | bytes 4202496 | tf_op jit(solution)/shard_map/gather | solution.py:175
  401.6 2.7 broadcast_select_fusion
  404.3 8.9 %all-to-all-start.2 = ((bf16[64,32,512]{2,1,0:T(8,128)(2,1)}), bf16[64,32,512]{2,1,0:T(8,128)(2,1)}, u32[]{:S(2)}, u32[]{:S(2)}) async-start(bf16[64,32,512]{2,1,0:T(8,128)(2,1)} %broadcast_select_fusion), calls=%async_computation.2 | async-start | bytes 4194304 | tf_op jit(solution)/shard_map/all_to_all | solution.py:177
  413.3 3.3 fusion.71
  416.6 6.7 fusion.75
  424.6 3.7 fusion.68
  428.4 81.7 %psum.23 = f32[512]{0:T(512)S(1)} all-reduce(f32[512]{0:T(512)S(1)} %get-tuple-element.119), channel_id=1, replica_groups=mesh['pts'=64,'rep'=4] {'pts','rep'}, use_global_device_ids=true, to_apply=%region_22.23 | all-reduce | flops 512 | bytes 4096 | tf_op jit(solution)/shard_map/psum | solution.py:180
  510.6 193.6 %all-reduce.3.cloned.1.call-done = (f32[512,1536]{1,0:T(8,128)}, f32[512,512]{1,0:T(8,128)}) async-done(((f32[512,1536]{1,0:T(8,128)}, f32[512,512]{1,0:T(8,128)}), (f32[512,1536]{1,0:T(8,128)}, f32[512,512]{1,0:T(8,128)})) %all-reduce.3.cloned.1.call-update) | async-done | bytes 4194320 | tf_op jit(solution)/shard_map/psum | solution.py:180
  704.2 2.3 broadcast_multiply_fusion.1
  706.5 3.8 broadcast_multiply_fusion
  710.3 11.3 %gather_fusion.1 = bf16[2048,512]{1,0:T(8,128)(2,1)} fusion(bf16[2048,512]{1,0:T(8,128)(2,1)} %bitcast.44, s32[2048]{0:T(1024)S(1)} %broadcast_clamp_fusion), kind=kCustom, calls=%fused_computation.1 | custom fusion | bytes 4202496 | tf_op jit(solution)/shard_map/gather | solution.py:179
  721.6 2.7 bitcast_select_fusion
  (145 shorter events, 105.4 us)
Async XLA Ops:
  7.2 41.4 %copy-start = (bf16[1,2048,512]{2,1,0:T(8,128)(2,1)S(1)}, bf16[1,2048,512]{2,1,0:T(8,128)(2,1)}, u32[]{:S(2)}) copy-start(bf16[1,2048,512]{2,1,0:T(8,128)(2,1)} %param.16) | copy-start | bytes 6291460
  8.7 19.2 %copy-start.4 = (s32[1,2048]{1,0:T(1,128)S(1)}, s32[1,2048]{1,0:T(1,128)}, u32[]{:S(2)}) copy-start(s32[1,2048]{1,0:T(1,128)} %param.18) | copy-start | bytes 24580
  37.6 22.0 %all-to-all-start = ((s32[64,32,1]{1,2,0:T(1,128)}), s32[64,32,1]{1,2,0:T(1,128)S(1)}, u32[]{:S(2)}, u32[]{:S(2)}) async-start(s32[64,32,1]{1,2,0:T(1,128)} %bitcast.21), calls=%async_computation | async-start | bytes 65536 | tf_op jit(solution)/shard_map/all_to_all | solution.py:128
  59.6 59.2 %all-to-all-start.1 = ((bf16[64,32,512]{2,1,0:T(8,128)(2,1)}), bf16[64,32,512]{2,1,0:T(8,128)(2,1)S(1)}, u32[]{:S(2)}, u32[]{:S(2)}) async-start(bf16[64,32,512]{2,1,0:T(8,128)(2,1)} %bitcast.182), calls=%async_computation.1 | async-start | bytes 4194304 | tf_op jit(solution)/shard_map/all_to_all | solution.py:127
  69.9 72.0 %copy-start.8 = (f32[512]{0:T(512)S(1)}, f32[512]{0:T(512)}, u32[]{:S(2)}) copy-start(f32[512]{0:T(512)} %param.20) | copy-start | bytes 6148
  141.1 1.4 copy-start.9
  142.5 3.6 copy-start.2
  142.5 3.6 copy-start.12
  146.1 53.4 %collective-permute-start = (bf16[1024,1536]{1,0:T(8,128)(2,1)}, bf16[1024,1536]{1,0:T(8,128)(2,1)}, u32[]{:S(2)}, u32[]{:S(2)}) collective-permute-start(bf16[1024,1536]{1,0:T(8,128)(2,1)} %convolution_convert_fusion.2), channel_id=1, source_target_pairs={{0,252},{4,0},{8,4},{12,8},{16,12},{20,16},{24,20},{28,24},{32,28}... | collective-permute-start | bytes 9437192 | tf_op jit(solution)/shard_map/ppermute | solution.py:15
  146.8 48.7 %collective-permute-start.2 = (bf16[1024,512]{1,0:T(8,128)(2,1)S(1)}, bf16[1024,512]{1,0:T(8,128)(2,1)}, u32[]{:S(2)}, u32[]{:S(2)}) collective-permute-start(bf16[1024,512]{1,0:T(8,128)(2,1)S(1)} %convolution_convert_fusion.3), channel_id=1, source_target_pairs={{0,252},{4,0},{8,4},{12,8},{16,12},{20,16},{24,20},{28,24},{32,28}... | collective-permute-start | bytes 3145736 | tf_op jit(solution)/shard_map/ppermute | solution.py:15
  345.1 41.0 %collective-permute-start.3 = (bf16[1024,1536]{0,1:T(8,128)(2,1)}, bf16[1024,1536]{0,1:T(8,128)(2,1)}, u32[]{:S(2)}, u32[]{:S(2)}) collective-permute-start(bf16[1024,1536]{0,1:T(8,128)(2,1)} %slice.55), channel_id=1, source_target_pairs={{0,4},{4,8},{8,12},{12,16},{16,20},{20,24},{24,28},{28,32},{32,36}... | collective-permute-start | bytes 9437192 | tf_op jit(solution)/shard_map/ppermute | solution.py:15
  385.2 6.1 copy-start.3
  385.2 28.1 %collective-permute-start.1 = (bf16[1024,512]{0,1:T(8,128)(2,1)}, bf16[1024,512]{0,1:T(8,128)(2,1)}, u32[]{:S(2)}, u32[]{:S(2)}) collective-permute-start(bf16[1024,512]{0,1:T(8,128)(2,1)} %bitcast.197), channel_id=1, source_target_pairs={{0,4},{4,8},{8,12},{12,16},{16,20},{20,24},{24,28},{28,32},{32,36}... | collective-permute-start | bytes 3145736 | tf_op jit(solution)/shard_map/ppermute | solution.py:15
  391.3 1.0 copy-start.6
  392.4 9.2 %copy-start.5 = (pred[64,32]{1,0:T(8,128)(4,1)S(1)}, pred[64,32]{1,0:T(8,128)(4,1)}, u32[]{:S(2)}) copy-start(pred[64,32]{1,0:T(8,128)(4,1)} %copy.52) | copy-start | bytes 6148
  404.3 9.0 %copy-start.10 = (bf16[8,1,1024,64]{2,3,1,0:T(8,128)(2,1)S(1)}, bf16[8,1,1024,64]{2,3,1,0:T(8,128)(2,1)}, u32[]{:S(2)}) copy-start(bf16[8,1,1024,64]{2,3,1,0:T(8,128)(2,1)} %get-tuple-element.84) | copy-start | bytes 3145732
  404.3 306.0 %all-to-all-start.2 = ((bf16[64,32,512]{2,1,0:T(8,128)(2,1)}), bf16[64,32,512]{2,1,0:T(8,128)(2,1)}, u32[]{:S(2)}, u32[]{:S(2)}) async-start(bf16[64,32,512]{2,1,0:T(8,128)(2,1)} %broadcast_select_fusion), calls=%async_computation.2 | async-start | bytes 4194304 | tf_op jit(solution)/shard_map/all_to_all | solution.py:177
  413.2 291.0 %all-reduce.3.cloned.1.call-start = ((), (), s32[]{:S(2)}) async-start(), calls=%async_computation.3 | async-start | bytes 8388608 | tf_op jit(solution)/shard_map/psum | solution.py:180
  423.3 0.7 copy-start.7
  423.3 1.2 copy-start.11
  423.3 1.4 copy-start.13
  710.3 14.0 %copy-start.1 = (bf16[1,2048,512]{2,1,0:T(8,128)(2,1)S(1)}, bf16[1,2048,512]{2,1,0:T(8,128)(2,1)}, u32[]{:S(2)}) copy-start(bf16[1,2048,512]{2,1,0:T(8,128)(2,1)} %param.16) | copy-start | bytes 6291460
Sparse Core Ops, SparseCore 0:
  423.4 280.7 all-reduce.2
where the time goes:
time: 742 us; the launch traced here: 732 us
  waiting for transfers between devices  287 us (39%)
  local copies, waits for them, and re-layouts  122 us (16%)
  matrix products  120 us (16%)
  blocking collectives  81.7 us (11%)
  other arithmetic  72.8 us (10%)
  starting transfers between devices  31.5 us (4%)
  between operations  16.2 us (2%)
    psum x1, waiting for transfers between devices, on_device(): lax.psum((grad_in, grad_out, grad_scale), ('pts', 'rep'))  194 us
    psum x1, blocking collectives, on_device(): lax.psum((grad_in, grad_out, grad_scale), ('pts', 'rep'))  81.7 us
    all_to_all x1, waiting for transfers between devices, on_device(): lax.all_to_all(outgoing, 'pts', split_axis=0, concat_axis=0, tiled=True)  47.5 us
    ppermute x4, waiting for transfers between devices, shifted(): return lax.ppermute(value, axis, pairs)  46.3 us
    dynamic_update_slice x1, local copies, waits for them, and re-layouts, on_device(): lax.dynamic_update_slice(jnp.zeros((row_count + PATCH, 3 * width), jnp.bf...  31.6 us
    scatter x1, local copies, waits for them, and re-layouts, on_device(): jnp.zeros((row_count, width), jnp.bfloat16).at[placed]  22.3 us
    dot_general x8, matrix products, head_forward(): jnp.einsum('gqk,gkd->gqd', attention, value_rows, preferred_element_type=...  20.9 us
    another operation x2, other arithmetic  18.3 us
  transfers between devices with their start and end apart: 8, of which 3 were waited for; matrix products, arithmetic and copies ran while one was open for 13% of the time, Pallas kernels for 0%

commit v1 on v0

--- a/solution.py
+++ b/solution.py
@@ -106,6 +106,10 @@
 def on_device(
     points, counts, hilbert_rank, patch_shift, norm_gain, project_in, project_out, cotangent
 ):
+
+    def treat_the_tables(q_in):
+        return lax.psum(lax.psum(q_in, "pts"), "rep")
+
     shard_count = lax.axis_size("pts")
     row_count = cotangent.shape[1]
     width = points.shape[2]
@@ -177,7 +181,7 @@
     arrived = lax.all_to_all(returning, "pts", split_axis=0, concat_axis=0, tiled=True)
     safe_target = jnp.clip(target, 0, shard_count * slot_size - 1)
     grad_points = jnp.where(live_slot[:, None], arrived[safe_target], jnp.zeros((), jnp.bfloat16))
-    summed_in, summed_out, summed_scale = lax.psum((grad_in, grad_out, grad_scale), ("pts", "rep"))
+    summed_in, summed_out, summed_scale = treat_the_tables((grad_in, grad_out, grad_scale))
     factor = 1.0 / math.sqrt(total * lax.axis_size("rep"))
     return (
         block_rows[None],

time: 742 us -> 808 us (1.089)
  the two profiles are of different devices: /device:TPU:97 before, /device:TPU:0 now
where the time goes in v1:
time: 808 us; the launch traced here: 797 us
  waiting for transfers between devices  304 us (38%)
  blocking collectives  138 us (17%)
  matrix products  121 us (15%)
  local copies, waits for them, and re-layouts  118 us (15%)
  other arithmetic  71.2 us (9%)
  starting transfers between devices  28 us (3%)
  between operations  16.1 us (2%)
    psum x2, waiting for transfers between devices, treat_the_tables(): return lax.psum(lax.psum(q_in, 'pts'), 'rep')  193 us
    psum x2, blocking collectives, treat_the_tables(): return lax.psum(lax.psum(q_in, 'pts'), 'rep')  138 us
    ppermute x4, waiting for transfers between devices, shifted(): return lax.ppermute(value, axis, pairs)  61.8 us
    all_to_all x1, waiting for transfers between devices, on_device(): lax.all_to_all(outgoing, 'pts', split_axis=0, concat_axis=0, tiled=True)  49.7 us
    dynamic_update_slice x1, local copies, waits for them, and re-layouts, on_device(): lax.dynamic_update_slice(jnp.zeros((row_count + PATCH, 3 * width), jnp.bf...  31.6 us
    scatter x1, local copies, waits for them, and re-layouts, on_device(): jnp.zeros((row_count, width), jnp.bfloat16).at[placed]  22.2 us
    dot_general x8, matrix products, head_forward(): jnp.einsum('gqk,gkd->gqd', attention, value_rows, preferred_element_type=...  20.9 us
    another operation x2, other arithmetic  18.3 us
  transfers between devices with their start and end apart: 9, of which 4 were waited for; matrix products, arithmetic and copies ran while one was open for 12% of the time, Pallas kernels for 0%

profile of v1, /device:TPU:0, one launch (start us, length us, event | category | flops | bytes accessed | tf_op | source)
XLA Modules:
  0.0 797.0 jit_solution(9242106345749315431)
XLA Ops:
  8.8 18.1 %reduce-window.6 = s32[64,16,128]{2,1,0:T(8,128)S(1)} reduce-window(s32[64,16,128]{2,1,0:T(8,128)S(1)} %fusion.81, s32[]{:T(128)} %constant.143.clone.1), window={size=1x1x128 pad=0_0x0_0x127_0}, to_apply=%region_0.1 | reduce-window | flops 16646144 | bytes 1048580 | tf_op jit(solution)/shard_map/reduce-window
  28.9 8.0 %scatter_custom_fusion = s32[2048]{0:T(1024)S(1)} fusion(s32[2048]{0:T(1024)S(1)} %bitcast.196, s32[2048]{0:T(1024)S(1)} %get-tuple-element.161, s32[]{:T(128)} %constant.142.clone.1), kind=kCustom, calls=%fused_computation.164 | custom fusion | bytes 8196 | tf_op jit(solution)/shard_map/scatter | solution.py:128
  37.6 10.2 %all-to-all-start = ((s32[64,32,1]{1,2,0:T(1,128)}), s32[64,32,1]{1,2,0:T(1,128)S(1)}, u32[]{:S(2)}, u32[]{:S(2)}) async-start(s32[64,32,1]{1,2,0:T(1,128)} %bitcast.21), calls=%async_computation | async-start | bytes 65536 | tf_op jit(solution)/shard_map/all_to_all | solution.py:132
  47.9 11.0 %scatter_custom_fusion.1 = bf16[2048,512]{1,0:T(8,128)(2,1)} fusion(s32[2048]{0:T(1024)S(1)} %bitcast.197, bf16[1,2048,512]{2,1,0:T(8,128)(2,1)S(1)} %copy-done, bf16[]{:T(256)} %constant.141.clone.1), kind=kCustom, calls=%fused_computation.88 | custom fusion | bytes 4194306 | tf_op jit(solution)/shard_map/scatter | solution.py:125
  58.9 10.3 %all-to-all-start.1 = ((bf16[64,32,512]{2,1,0:T(8,128)(2,1)}), bf16[64,32,512]{2,1,0:T(8,128)(2,1)S(1)}, u32[]{:S(2)}, u32[]{:S(2)}) async-start(bf16[64,32,512]{2,1,0:T(8,128)(2,1)} %bitcast.183), calls=%async_computation.1 | async-start | bytes 4194304 | tf_op jit(solution)/shard_map/all_to_all | solution.py:131
  70.6 49.7 %all-to-all-done.1 = bf16[64,32,512]{2,1,0:T(8,128)(2,1)S(1)} async-done(((bf16[64,32,512]{2,1,0:T(8,128)(2,1)}), bf16[64,32,512]{2,1,0:T(8,128)(2,1)S(1)}, u32[]{:S(2)}, u32[]{:S(2)}) %all-to-all-start.1) | async-done | bytes 2097184 | tf_op jit(solution)/shard_map/all_to_all | solution.py:131
  120.3 22.2 %scatter_custom_fusion.2 = bf16[1024,512]{1,0:T(8,128)(2,1)S(1)} fusion(s32[2048]{0:T(1024)S(1)} %bitcast.195, bf16[2048,512]{1,0:T(8,128)(2,1)S(1)} %bitcast.185, bf16[]{:T(256)} %constant.141.clone.1), kind=kCustom, calls=%fused_computation.113 | custom fusion | bytes 1048578 | tf_op jit(solution)/shard_map/scatter | solution.py:135
  144.0 3.5 convolution_convert_fusion.2
  150.2 44.3 %collective-permute-done.2 = bf16[1024,512]{1,0:T(8,128)(2,1)} collective-permute-done((bf16[1024,512]{1,0:T(8,128)(2,1)S(1)}, bf16[1024,512]{1,0:T(8,128)(2,1)}, u32[]{:S(2)}, u32[]{:S(2)}) %collective-permute-start.2) | collective-permute-done | bytes 1048608 | tf_op jit(solution)/shard_map/ppermute | solution.py:15
  194.5 2.6 fusion.69
  198.5 6.7 fusion.50
  205.2 4.6 copy.47
  209.8 3.7 slice_bitcast_fusion
  217.3 2.7 copy.48
  220.0 85.2 %while.23 = (s32[]{:T(128)}, bf16[8,3,1,1024,64]{3,4,0,1,2:T(8,128)(2,1)}, bf16[8,1,1024,64]{3,2,1,0:T(8,128)(2,1)}, bf16[8,1,1024,64]{3,2,1,0:T(8,128)(2,1)S(1)...) while((s32[]{:T(128)}, bf16[8,3,1,1024,64]{3,4,0,1,2:T(8,128)(2,1)}, ...), condition=%wide.region_16.17_spmd, body=%wide.region_12.16_spmd.sunk | while | flops 694481920 | bytes 38451300 | solution.py:89
  224.3 2.0 multiply_reduce_fusion.9
  234.9 2.0 multiply_reduce_fusion.9
  245.6 2.0 multiply_reduce_fusion.9
  256.2 2.0 multiply_reduce_fusion.9
  266.8 2.0 multiply_reduce_fusion.9
  277.5 2.0 multiply_reduce_fusion.9
  288.1 2.0 multiply_reduce_fusion.9
  305.1 3.5 broadcast_in_dim.94
  308.6 31.6 %dynamic_update_slice.11 = bf16[2048,1536]{0,1:T(8,128)(2,1)} dynamic-update-slice(bf16[2048,1536]{0,1:T(8,128)(2,1)} %broadcast_in_dim.94, bf16[1024,1536]{0,1:T(8,128)(2,1)} %bitcast.184, s32[]{:T(128)S(6)} %select_n.180, s32[]{:T(128)} %constant.143.clone.1) | dynamic-update-slice | bytes 6291460 | tf_op jit(solution)/shard_map/dynamic_update_slice | solution.py:162
  340.2 3.9 slice.55
  345.5 40.1 %while.22 = (s32[]{:T(128)}, bf16[8,1,1024,64]{2,3,1,0:T(8,128)(2,1)}, bf16[8,1,1024,64]{3,2,1,0:T(8,128)(2,1)}, bf16[8,1,1024,64]{3,2,1,0:T(8,128)(2,1)S(1)}, bf16[8,1,1024,64]{3,2,1,0:T(8,128)(2,1)}, /*index=5*/s32[]{:T(128)}) while((s32[]{:T(128)}, bf16[8,1,1024,64]{2,3,1,0:T(8,128)(2,1)}, bf16[8,1,1024,64]{3,2,1,0:T(8,128)(2,1)}, ...), condition=%wide.region_11.12_spmd, body=%wide.region_8.11_spmd.sunk | while | flops 277936128 | bytes 13523021 | solution.py:53
  347.9 2.6 fusion.121
  352.9 2.6 fusion.121
  357.9 2.6 fusion.121
  362.9 2.6 fusion.121
  367.9 2.6 fusion.121
  373.0 2.6 fusion.121
  378.0 2.6 fusion.121
  383.0 2.6 fusion.121
  385.8 17.5 %collective-permute-done.1 = bf16[1024,512]{0,1:T(8,128)(2,1)S(1)} collective-permute-done((bf16[1024,512]{0,1:T(8,128)(2,1)}, bf16[1024,512]{0,1:T(8,128)(2,1)S(1)}, u32[]{:S(2)}, u32[]{:S(2)}) %collective-permute-start.1) | collective-permute-done | bytes 1048608 | tf_op jit(solution)/shard_map/ppermute | solution.py:15
  403.3 3.7 fusion.71
  407.0 6.7 fusion.75
  413.8 5.3 fusion.63
  420.1 9.2 %gather_fusion = bf16[2048,512]{1,0:T(8,128)(2,1)} fusion(bf16[1024,512]{1,0:T(8,128)(2,1)S(1)} %fusion.62, s32[2048]{0:T(1024)S(1)} %broadcast_clamp_fusion.1), kind=kCustom, calls=%fused_computation | custom fusion | bytes 4202496 | tf_op jit(solution)/shard_map/gather | solution.py:179
  429.3 2.8 broadcast_select_fusion
  432.1 4.7 all-to-all-start.2
  436.8 192.7 %all-reduce.5.cloned.1.call-done = (f32[512,1536]{1,0:T(8,128)}, f32[512,512]{1,0:T(8,128)}) async-done(((f32[512,1536]{1,0:T(8,128)}, f32[512,512]{1,0:T(8,128)}), (f32[512,1536]{1,0:T(8,128)}, f32[512,512]{1,0:T(8,128)})) %all-reduce.5.cloned.1.call-update) | async-done | bytes 4194320 | tf_op jit(solution)/shard_map/psum | solution.py:111
  630.2 4.0 fusion.68
  634.2 127.5 %psum.46 = f32[512]{0:T(512)S(1)} all-reduce(f32[512]{0:T(512)S(1)} %get-tuple-element.119), channel_id=1, replica_groups=mesh['pts'=64,'rep'=4] {'pts'}, use_global_device_ids=true, to_apply=%region_24.25 | all-reduce | flops 512 | bytes 4096 | tf_op jit(solution)/shard_map/psum | solution.py:111
  761.7 10.5 %psum.47 = f32[512]{0:T(512)S(1)} all-reduce(f32[512]{0:T(512)S(1)} %psum.46), channel_id=1, replica_groups=mesh['pts'=64,'rep'=4] {'rep'}, use_global_device_ids=true, to_apply=%region_25.26 | all-reduce | flops 512 | bytes 4096 | tf_op jit(solution)/shard_map/psum | solution.py:111
  772.7 9.2 %gather_fusion.1 = bf16[2048,512]{1,0:T(8,128)(2,1)} fusion(bf16[2048,512]{1,0:T(8,128)(2,1)S(1)} %bitcast.180, s32[2048]{0:T(1024)S(1)} %broadcast_clamp_fusion), kind=kCustom, calls=%fused_computation.1 | custom fusion | bytes 4202496 | tf_op jit(solution)/shard_map/gather | solution.py:183
  781.9 2.7 bitcast_select_fusion
  784.7 4.0 broadcast_multiply_fusion
  (143 shorter events, 108.1 us)
Async XLA Ops:
  7.2 40.7 %copy-start = (bf16[1,2048,512]{2,1,0:T(8,128)(2,1)S(1)}, bf16[1,2048,512]{2,1,0:T(8,128)(2,1)}, u32[]{:S(2)}) copy-start(bf16[1,2048,512]{2,1,0:T(8,128)(2,1)} %param.16) | copy-start | bytes 6291460
  8.7 19.2 %copy-start.5 = (s32[1,2048]{1,0:T(1,128)S(1)}, s32[1,2048]{1,0:T(1,128)}, u32[]{:S(2)}) copy-start(s32[1,2048]{1,0:T(1,128)} %param.18) | copy-start | bytes 24580
  37.6 21.2 %all-to-all-start = ((s32[64,32,1]{1,2,0:T(1,128)}), s32[64,32,1]{1,2,0:T(1,128)S(1)}, u32[]{:S(2)}, u32[]{:S(2)}) async-start(s32[64,32,1]{1,2,0:T(1,128)} %bitcast.21), calls=%async_computation | async-start | bytes 65536 | tf_op jit(solution)/shard_map/all_to_all | solution.py:132
  58.9 61.5 %all-to-all-start.1 = ((bf16[64,32,512]{2,1,0:T(8,128)(2,1)}), bf16[64,32,512]{2,1,0:T(8,128)(2,1)S(1)}, u32[]{:S(2)}, u32[]{:S(2)}) async-start(bf16[64,32,512]{2,1,0:T(8,128)(2,1)} %bitcast.183), calls=%async_computation.1 | async-start | bytes 4194304 | tf_op jit(solution)/shard_map/all_to_all | solution.py:131
  69.2 74.2 %copy-start.7 = (f32[512]{0:T(512)S(1)}, f32[512]{0:T(512)}, u32[]{:S(2)}) copy-start(f32[512]{0:T(512)} %param.20) | copy-start | bytes 6148
  69.2 560.3 %all-reduce.5.cloned.1.call-start = ((), (), s32[]{:S(2)}) async-start(), calls=%async_computation.3 | async-start | bytes 8388608 | tf_op jit(solution)/shard_map/psum | solution.py:111
  142.6 1.4 copy-start.8
  144.0 4.2 copy-start.2
  144.0 4.2 copy-start.10
  147.5 50.9 %collective-permute-start = (bf16[1024,1536]{1,0:T(8,128)(2,1)}, bf16[1024,1536]{1,0:T(8,128)(2,1)}, u32[]{:S(2)}, u32[]{:S(2)}) collective-permute-start(bf16[1024,1536]{1,0:T(8,128)(2,1)} %convolution_convert_fusion.2), channel_id=1, source_target_pairs={{0,252},{4,0},{8,4},{12,8},{16,12},{20,16},{24,20},{28,24},{32,28}... | collective-permute-start | bytes 9437192 | tf_op jit(solution)/shard_map/ppermute | solution.py:15
  149.0 45.5 %collective-permute-start.2 = (bf16[1024,512]{1,0:T(8,128)(2,1)S(1)}, bf16[1024,512]{1,0:T(8,128)(2,1)}, u32[]{:S(2)}, u32[]{:S(2)}) collective-permute-start(bf16[1024,512]{1,0:T(8,128)(2,1)S(1)} %convolution_convert_fusion.3), channel_id=1, source_target_pairs={{0,252},{4,0},{8,4},{12,8},{16,12},{20,16},{24,20},{28,24},{32,28}... | collective-permute-start | bytes 3145736 | tf_op jit(solution)/shard_map/ppermute | solution.py:15
  344.1 63.0 %collective-permute-start.3 = (bf16[1024,1536]{0,1:T(8,128)(2,1)}, bf16[1024,1536]{0,1:T(8,128)(2,1)}, u32[]{:S(2)}, u32[]{:S(2)}) collective-permute-start(bf16[1024,1536]{0,1:T(8,128)(2,1)} %slice.55), channel_id=1, source_target_pairs={{0,4},{4,8},{8,12},{12,16},{16,20},{20,24},{24,28},{28,32},{32,36}... | collective-permute-start | bytes 9437192 | tf_op jit(solution)/shard_map/ppermute | solution.py:15
  385.6 17.8 %collective-permute-start.1 = (bf16[1024,512]{0,1:T(8,128)(2,1)}, bf16[1024,512]{0,1:T(8,128)(2,1)S(1)}, u32[]{:S(2)}, u32[]{:S(2)}) collective-permute-start(bf16[1024,512]{0,1:T(8,128)(2,1)} %bitcast.198), channel_id=1, source_target_pairs={{0,4},{4,8},{8,12},{12,16},{16,20},{20,24},{24,28},{28,32},{32,36}... | collective-permute-start | bytes 3145736 | tf_op jit(solution)/shard_map/ppermute | solution.py:15
  403.3 3.7 copy-start.9
  413.8 5.3 copy-start.3
  432.1 340.7 %all-to-all-start.2 = ((bf16[64,32,512]{2,1,0:T(8,128)(2,1)}), bf16[64,32,512]{2,1,0:T(8,128)(2,1)S(1)}, u32[]{:S(2)}, u32[]{:S(2)}) async-start(bf16[64,32,512]{2,1,0:T(8,128)(2,1)} %broadcast_select_fusion), calls=%async_computation.2 | async-start | bytes 4194304 | tf_op jit(solution)/shard_map/all_to_all | solution.py:181
  436.8 347.9 %all-reduce.7.cloned.1.call-start = ((), (), s32[]{:S(2)}) async-start(), calls=%async_computation.4 | async-start | bytes 8388608 | tf_op jit(solution)/shard_map/psum | solution.py:111
  629.5 0.7 copy-start.6
  784.7 4.0 copy-start.4
  784.7 5.0 copy-start.1
Sparse Core Ops, SparseCore 0:
  413.9 215.5 all-reduce.4
  632.0 96.7 all-reduce.6
